TPU v7x, 32 devices: a whole 2x2x4 slice. The times are simulated.
32 devices in a mesh: dp: 4 (over x, core), ctx: 8 (over z, y).
Axes of the slice: x: 2, y: 2, z: 4, core: 2. Of those that a mesh axis runs over, the one named last changes fastest.
Arguments:
- merged_grad: bfloat16 [4096, 1792], P(('dp', 'ctx')), may hold values from -6 to 6
- merged_owner: int32 [4096, 1], P(('dp', 'ctx')), may hold values from 0 to 7; in each aligned block of 128 rows (0 to 127, 128 to 255, ...) at most 32 rows name the same one
- merger_pre: bfloat16 [8192, 2560], P(('dp', 'ctx')), may hold values from -6 to 6
- fc2_weight: bfloat16 [2560, 1792], P('ctx'), may hold values from -0.125 to 0.125
- query: bfloat16 [8192, 1280], P(('dp', 'ctx')), may hold values from -32 to 32
- key_states: bfloat16 [8192, 1280], P(('dp', 'ctx')), may hold values from -32 to 32
- value_states: bfloat16 [8192, 1280], P(('dp', 'ctx')), may hold values from -6 to 6
- out_grad: bfloat16 [8192, 1280], P(('dp', 'ctx')), may hold values from -6 to 6
- position: int32 [2, 8192], P(None, ('dp', 'ctx')), may hold values from 0 to 63, as said below
Outputs:
- hidden_grad: bfloat16 [8192, 2560], P(('dp', 'ctx'))
- weight_grad: float32 [2560, 1792], P('ctx', 'dp')
- query_grad: bfloat16 [8192, 1280], P(('dp', 'ctx'))
- key_grad: bfloat16 [8192, 1280], P(('dp', 'ctx'))
- value_grad: bfloat16 [8192, 1280], P(('dp', 'ctx'))
Inputs may be any that keep to these rules, and one draw needn't show every extreme that they name: `merged_owner`: in each device's block of 128 rows no owner is named more than 32 times. `position`: each window of 64 consecutive patches covers an aligned square of 8 by 8 grid positions, row by row.
All inputs are finite; a program needn't handle non-finite values.
Results may differ from a plain program's by a relative error of at most 0.0017.
The roundings to bfloat16 on the way count: a program that leaves them out, or rounds other values in their place, can miss the bound.
Values may be sent and summed in bfloat16 or wider, within the bound.
A program may use at most 128 MiB of HBM per device.

v0:
```python
import math

import jax
import jax.numpy as jnp
from jax import lax
from jax.sharding import PartitionSpec as P

D = 1280
HEADS = 16
HEAD = 80
WIN = 64


def entering(part, axis, combine, identity):
    place = lax.axis_index(axis)
    gathered = lax.all_gather(part, axis)
    state = jnp.zeros_like(part) + jnp.asarray(identity, part.dtype)

    def one(hop, state):
        return combine(state, lax.dynamic_index_in_dim(gathered, hop, 0, False))

    return lax.fori_loop(0, place, one, state)


def rope_angles(position, head_size):
    quarter = head_size // 4
    freq = 1.0 / 10000.0 ** (jnp.arange(quarter, dtype=jnp.float32) * (4.0 / head_size))
    rows = position[0].astype(jnp.float32)[:, None] * freq[None, :]
    cols = position[1].astype(jnp.float32)[:, None] * freq[None, :]
    return jnp.concatenate([rows, cols], axis=1)


def rotate(values, angles, sign):
    half = values.shape[-1] // 2
    cosine = jnp.cos(angles)[:, None, :]
    sine = sign * jnp.sin(angles)[:, None, :]
    first = values[..., :half]
    second = values[..., half:]
    return jnp.concatenate(
        [first * cosine - second * sine, second * cosine + first * sine], axis=-1
    )


def attention_block(query, key_states, value_states, out_grad, position):
    count = query.shape[0]
    windows = count // WIN
    angles = rope_angles(position, HEAD)
    shaped = (count, HEADS, HEAD)
    grouped = (windows, WIN, HEADS, HEAD)
    q_rot = (
        rotate(query.astype(jnp.float32).reshape(shaped), angles, 1.0)
        .astype(jnp.bfloat16)
        .reshape(grouped)
    )
    k_rot = (
        rotate(key_states.astype(jnp.float32).reshape(shaped), angles, 1.0)
        .astype(jnp.bfloat16)
        .reshape(grouped)
    )
    v_win = value_states.reshape(grouped)
    g_win = out_grad.reshape(grouped)
    factor = HEAD ** (-0.5)
    f32 = jnp.float32
    scores = jnp.einsum("wqhd,wkhd->whqk", q_rot, k_rot, preferred_element_type=f32) * factor
    probs = jax.nn.softmax(scores, axis=-1)
    probs_b = probs.astype(jnp.bfloat16)
    output = jnp.einsum("whqk,wkhd->wqhd", probs_b, v_win, preferred_element_type=f32)
    value_grad = jnp.einsum("whqk,wqhd->wkhd", probs_b, g_win, preferred_element_type=f32).astype(
        jnp.bfloat16
    )
    prob_grad = jnp.einsum("wqhd,wkhd->whqk", g_win, v_win, preferred_element_type=f32)
    delta = jnp.transpose(jnp.sum(g_win.astype(f32) * output, axis=-1), (0, 2, 1))[..., None]
    score_grad = (probs * (prob_grad - delta)).astype(jnp.bfloat16)
    q_grad = jnp.einsum("whqk,wkhd->wqhd", score_grad, k_rot, preferred_element_type=f32) * factor
    k_grad = jnp.einsum("whqk,wqhd->wkhd", score_grad, q_rot, preferred_element_type=f32) * factor
    query_grad = rotate(q_grad.reshape(shaped), angles, -1.0).astype(jnp.bfloat16).reshape(count, D)
    key_grad = rotate(k_grad.reshape(shaped), angles, -1.0).astype(jnp.bfloat16).reshape(count, D)
    return (query_grad, key_grad, value_grad.reshape(count, D))


def add_counts(earlier, later):
    return earlier + later


def shards(
    merged_grad,
    merged_owner,
    merger_pre,
    fc2_weight,
    query,
    key_states,
    value_states,
    out_grad,
    position,
):
    rows_here = merged_grad.shape[0]
    owners_count = lax.axis_size("ctx")
    replicas = lax.axis_size("dp")
    slots = merger_pre.shape[0]
    capacity = slots // owners_count
    owner = merged_owner[:, 0]
    peers = jnp.arange(owners_count, dtype=jnp.int32)
    onehot = (owner[:, None] == peers[None, :]).astype(jnp.int32)
    counts = jnp.sum(onehot, axis=0, dtype=jnp.int32)
    running = jnp.cumsum(onehot, axis=0, dtype=jnp.int32)
    local_rank = jnp.sum(running * onehot, axis=1, dtype=jnp.int32) - 1
    before = entering(counts, "ctx", add_counts, jnp.zeros_like(counts))
    slot_of_row = jnp.sum(onehot * before[None, :], axis=1, dtype=jnp.int32) + local_rank
    target = owner * capacity + local_rank
    places = jnp.arange(owners_count * capacity, dtype=jnp.int32)
    select = places[:, None] == target[None, :]
    outgoing = jnp.dot(select.astype(jnp.bfloat16), merged_grad, preferred_element_type=jnp.float32)
    outgoing = outgoing.astype(jnp.bfloat16).reshape(owners_count, capacity, merged_grad.shape[1])
    outgoing_slot = (
        jnp.sum(jnp.where(select, slot_of_row[None, :] + 1, 0), axis=1, dtype=jnp.int32) - 1
    )
    outgoing_slot = outgoing_slot.reshape(owners_count, capacity)
    incoming, incoming_slot = (
        lax.all_to_all(outgoing, "ctx", split_axis=0, concat_axis=0, tiled=True),
        lax.all_to_all(outgoing_slot, "ctx", split_axis=0, concat_axis=0, tiled=True),
    )
    landing = jnp.arange(slots, dtype=jnp.int32)[:, None] == incoming_slot.reshape(1, slots)
    slotted = jnp.dot(
        landing.astype(jnp.bfloat16),
        incoming.reshape(slots, -1),
        preferred_element_type=jnp.float32,
    )
    slotted = slotted.astype(jnp.bfloat16)
    pre = merger_pre.astype(jnp.float32)
    cdf = 0.5 * (1.0 + lax.erf(pre * 0.5**0.5))
    act = (pre * cdf).astype(jnp.bfloat16)
    slope = cdf + pre * jnp.exp(-0.5 * pre * pre) * (2.0 * math.pi) ** (-0.5)
    linear = lax.dot_general(
        slotted,
        lax.all_gather(fc2_weight, "ctx", axis=0, tiled=True),
        (((1,), (1,)), ((), ())),
        preferred_element_type=jnp.float32,
    )
    hidden_grad = (linear * slope).astype(jnp.bfloat16)
    factor = (rows_here * owners_count * replicas) ** (-0.5)
    whole = lax.dot_general(
        act, slotted, (((0,), (0,)), ((), ())), preferred_element_type=jnp.float32
    )
    partial_dp = lax.psum_scatter(whole, "dp", scatter_dimension=1, tiled=True)
    summed = lax.psum_scatter(partial_dp, "ctx", scatter_dimension=0, tiled=True)
    weight_grad = summed * factor
    query_grad, key_grad, value_grad = attention_block(
        query, key_states, value_states, out_grad, position
    )
    return (hidden_grad, weight_grad, query_grad, key_grad, value_grad)


def solution(mesh):
    return jax.shard_map(
        shards,
        mesh=mesh,
        in_specs=(
            P(("dp", "ctx"), None),
            P(("dp", "ctx"), None),
            P(("dp", "ctx"), None),
            P("ctx", None),
            P(("dp", "ctx"), None),
            P(("dp", "ctx"), None),
            P(("dp", "ctx"), None),
            P(("dp", "ctx"), None),
            P(None, ("dp", "ctx")),
        ),
        out_specs=(
            P(("dp", "ctx"), None),
            P("ctx", "dp"),
            P(("dp", "ctx"), None),
            P(("dp", "ctx"), None),
            P(("dp", "ctx"), None),
        ),
        check_vma=False,
    )
```

profile of v0, /device:TPU:0, one launch (start us, length us, event | category | flops | bytes accessed | tf_op | source)
XLA Modules:
  0.0 323.0 jit_solution(4258777016265018463)
XLA Ops:
  11.7 13.1 %all-reduce = s32[64]{0:T(128)S(1)} all-reduce(s32[64]{0:T(128)S(1)} %dynamic-update-slice), channel_id=2, replica_groups=mesh['dp'=4,'ctx'=8] {'ctx'}, use_global_device_ids=true, to_apply=%add | all-reduce | flops 64 | bytes 512
  27.4 3.3 %all-to-all-start = ((s32[8,1,32]{2,1,0:T(1,128)}), s32[8,1,32]{2,1,0:T(1,128)S(1)}, u32[]{:S(2)}, u32[]{:S(2)}) async-start(s32[8,1,32]{2,1,0:T(1,128)} %sub.40), calls=%async_computation | async-start | bytes 8192 | tf_op jit(solution)/shard_map/all_to_all | solution.py:120
  32.0 5.0 %all-to-all-done = s32[8,1,32]{2,1,0:T(1,128)S(1)} async-done(((s32[8,1,32]{2,1,0:T(1,128)}), s32[8,1,32]{2,1,0:T(1,128)S(1)}, u32[]{:S(2)}, u32[]{:S(2)}) %all-to-all-start) | async-done | bytes 1056 | tf_op jit(solution)/shard_map/all_to_all | solution.py:120
  37.0 3.6 %all-to-all-start.1 = ((bf16[8,32,1792]{2,1,0:T(8,128)(2,1)}), bf16[8,32,1792]{2,1,0:T(8,128)(2,1)S(1)}, u32[]{:S(2)}, u32[]{:S(2)}) async-start(bf16[8,32,1792]{2,1,0:T(8,128)(2,1)} %bitcast.3), calls=%async_computation.1 | async-start | bytes 1835008 | tf_op jit(solution)/shard_map/all_to_all | solution.py:119
  41.9 18.0 %all-to-all-done.1 = bf16[8,32,1792]{2,1,0:T(8,128)(2,1)S(1)} async-done(((bf16[8,32,1792]{2,1,0:T(8,128)(2,1)}), bf16[8,32,1792]{2,1,0:T(8,128)(2,1)S(1)}, u32[]{:S(2)}, u32[]{:S(2)}) %all-to-all-start.1) | async-done | bytes 917536 | tf_op jit(solution)/shard_map/all_to_all | solution.py:119
  60.4 10.3 %fusion.12 = f32[2560,1792]{0,1:T(8,128)} fusion(bf16[256,1792]{1,0:T(8,128)(2,1)S(1)} %convolution_convert_fusion.1, bf16[256,2560]{1,0:T(8,128)(2,1)} %param.13), kind=kOutput, calls=%fused_computation.28 | convolution fusion | flops 2352742400 | bytes 20578304 | tf_op jit(solution)/shard_map/dot_general | solution.py:141
  71.3 132.9 %reduce-scatter.5.cloned.1.call-done = f32[2560,448]{0,1:T(8,128)} async-done(((f32[2560,1792]{0,1:T(8,128)}), f32[2560,448]{0,1:T(8,128)}) %reduce-scatter.5.cloned.1.call-update) | async-done | bytes 4587536 | tf_op jit(solution)/shard_map/reduce_scatter | solution.py:144
  204.2 5.7 %copy.95 = f32[2560,448]{1,0:T(8,128)} copy(f32[2560,448]{0,1:T(8,128)} %reduce-scatter.5.cloned.1.call-done) | data formatting | bytes 9175040
  211.0 2.5 reshape.187
  213.6 2.5 reshape.186
  224.5 2.4 concatenate.45
  226.9 2.4 copy.73
  230.4 2.3 copy.72
  232.7 4.6 %fusion.39 = (f32[4,16,64]{2,1,0:T(8,128)S(1)}, f32[4,16,64,64]{2,3,1,0:T(8,128)}) fusion(bf16[4,64,16,40]{3,1,2,0:T(8,128)(2,1)S(1)} %copy.70, bf16[4,64,16,40]{3,1,2,0:T(8,128)(2,1)S(1)} %copy.69, bf16[4,64,16,40]{3,1,2,0:T(8,128)(2,1)} %copy.73, bf16[4,64,16,40]{3,1,2,0:T(8,128)(2,1)} %copy.72), kind=kOutput, calls=%fused_computation.79 | convolution fusion | flops 45350976 | bytes 2375680 | tf_op jit(solution)/shard_map/sub | solution.py:65
  237.3 3.4 %fusion.9 = f32[4,64,16]{1,2,0:T(8,128)S(1)} fusion(bf16[4,64,16,80]{3,2,1,0:T(8,128)(2,1)} %reshape.187, bf16[4,64,16,80]{3,2,1,0:T(8,128)(2,1)} %reshape.186, f32[4,16,64,64]{2,3,1,0:T(8,128)} %get-tuple-element.85, f32[4,16,64]{2,1,0:T(8,128)S(1)} %get-tuple-element.84), kind=kOutput, calls=%fused_computation.19 | convolution fusion | flops 43446272 | bytes 2392064 | tf_op jit(solution)/shard_map/whqk,wkhd->wqhd/dot_general | solution.py:67
  244.7 2.1 fusion.37
  246.8 3.3 %copy.100 = f32[256,16,40]{0,2,1:T(8,128)} copy(f32[256,16,40]{2,1,0:T(8,128)} %get-tuple-element.61) | data formatting | bytes 1310720
  252.0 2.8 multiply_bitcast_fusion.1
  256.0 2.1 fusion.38
  258.1 3.6 %copy.97 = f32[256,16,40]{0,2,1:T(8,128)} copy(f32[256,16,40]{2,1,0:T(8,128)} %get-tuple-element.64) | data formatting | bytes 1310720
  267.8 2.4 fusion.11
  270.9 2.0 reshape.190
  272.9 8.0 %fusion.1 = bf16[256,2560]{1,0:T(8,128)(2,1)} fusion(bf16[256,1792]{1,0:T(8,128)(2,1)S(1)} %convolution_convert_fusion.1, bf16[2560,1792]{1,0:T(8,128)(2,1)} %all-gather.3.cloned.1.call-done, bf16[256,2560]{1,0:T(8,128)(2,1)} %param.13), kind=kOutput, calls=%fused_computation.8 | convolution fusion | flops 2356019200 | bytes 12713984 | tf_op jit(solution)/shard_map/dot_general | solution.py:133
  280.9 32.1 %reduce-scatter.7.cloned.1.call-done = f32[320,448]{1,0:T(8,128)} async-done(((f32[2560,448]{1,0:T(8,128)}), f32[320,448]{1,0:T(8,128)}) %reduce-scatter.7.cloned.1.call-update) | async-done | bytes 573456
  (82 shorter events, 36.1 us)
Async XLA Ops:
  8.0 22.7 %copy-start = (bf16[128,1792]{1,0:T(8,128)(2,1)S(1)}, bf16[128,1792]{1,0:T(8,128)(2,1)}, u32[]{:S(2)}) copy-start(bf16[128,1792]{1,0:T(8,128)(2,1)} %param.11) | copy-start | bytes 1376260
  27.4 9.7 %all-to-all-start = ((s32[8,1,32]{2,1,0:T(1,128)}), s32[8,1,32]{2,1,0:T(1,128)S(1)}, u32[]{:S(2)}, u32[]{:S(2)}) async-start(s32[8,1,32]{2,1,0:T(1,128)} %sub.40), calls=%async_computation | async-start | bytes 8192 | tf_op jit(solution)/shard_map/all_to_all | solution.py:120
  37.0 22.9 %all-to-all-start.1 = ((bf16[8,32,1792]{2,1,0:T(8,128)(2,1)}), bf16[8,32,1792]{2,1,0:T(8,128)(2,1)S(1)}, u32[]{:S(2)}, u32[]{:S(2)}) async-start(bf16[8,32,1792]{2,1,0:T(8,128)(2,1)} %bitcast.3), calls=%async_computation.1 | async-start | bytes 1835008 | tf_op jit(solution)/shard_map/all_to_all | solution.py:119
  40.6 163.6 %reduce-scatter.5.cloned.1.call-start = ((), (), s32[]{:S(2)}) async-start(), calls=%async_computation.5 | async-start | bytes 22937600 | tf_op jit(solution)/shard_map/reduce_scatter | solution.py:144
  70.7 202.3 %all-gather.3.cloned.1.call-start = ((), (), s32[]{:S(2)}) async-start(), calls=%async_computation.4 | async-start | bytes 10321920 | tf_op jit(solution)/shard_map/all_gather | solution.py:135
  71.2 241.8 %reduce-scatter.7.cloned.1.call-start = ((), (), s32[]{:S(2)}) async-start(), calls=%async_computation.6 | async-start | bytes 5898240
  209.9 1.1 copy-start.9
  211.0 2.5 copy-start.10
  213.6 2.5 copy-start.11
  216.5 1.7 copy-start.12
  221.7 11.0 %copy-start.3 = (bf16[4,64,16,40]{3,1,2,0:T(8,128)(2,1)}, bf16[4,64,16,40]{3,1,2,0:T(8,128)(2,1)S(1)}, u32[]{:S(2)}) copy-start(bf16[4,64,16,40]{3,1,2,0:T(8,128)(2,1)S(1)} %copy.70) | copy-start | bytes 983044
  224.5 8.2 %copy-start.4 = (bf16[4,64,16,40]{3,1,2,0:T(8,128)(2,1)}, bf16[4,64,16,40]{3,1,2,0:T(8,128)(2,1)S(1)}, u32[]{:S(2)}) copy-start(bf16[4,64,16,40]{3,1,2,0:T(8,128)(2,1)S(1)} %copy.69) | copy-start | bytes 983044
  237.3 3.4 %copy-start.7 = (bf16[4,64,16,80]{3,2,1,0:T(8,128)(2,1)S(1)}, bf16[4,64,16,80]{3,2,1,0:T(8,128)(2,1)}, u32[]{:S(2)}) copy-start(bf16[4,64,16,80]{3,2,1,0:T(8,128)(2,1)} %reshape.186) | copy-start | bytes 1966084
  237.3 3.5 %copy-start.8 = (bf16[4,64,16,80]{3,2,1,0:T(8,128)(2,1)S(1)}, bf16[4,64,16,80]{3,2,1,0:T(8,128)(2,1)}, u32[]{:S(2)}) copy-start(bf16[4,64,16,80]{3,2,1,0:T(8,128)(2,1)} %reshape.187) | copy-start | bytes 1966084
  237.3 3.7 %copy-start.13 = (f32[4,16,64,64]{2,3,1,0:T(8,128)S(1)}, f32[4,16,64,64]{2,3,1,0:T(8,128)}, u32[]{:S(2)}) copy-start(f32[4,16,64,64]{2,3,1,0:T(8,128)} %get-tuple-element.85) | copy-start | bytes 3145732
  241.0 1.2 copy-start.5
  241.0 1.6 copy-start.6
  242.5 1.0 copy-start.2
  272.9 42.6 %copy-start.1 = (bf16[128,1792]{1,0:T(8,128)(2,1)S(1)}, bf16[128,1792]{1,0:T(8,128)(2,1)}, u32[]{:S(2)}) copy-start(bf16[128,1792]{1,0:T(8,128)(2,1)} %param.11) | copy-start | bytes 1376260
Sparse Core Ops, SparseCore 0:
  70.8 133.3 reduce-scatter.4
Sparse Core Ops, SparseCore 1:
  73.3 132.6 all-gather.2
  210.0 103.0 reduce-scatter.6
where the time goes:
time: 324 us; the launch traced here: 323 us
  waiting for transfers between devices  189 us (58%)
  local copies, waits for them, and re-layouts  55.2 us (17%)
  matrix products  34.7 us (11%)
  between operations  16.4 us (5%)
  blocking collectives  13.1 us (4%)
  other arithmetic  7.9 us (2%)
  starting transfers between devices  6.99 us (2%)
    reduce_scatter x1, waiting for transfers between devices, shards(): partial_dp = lax.psum_scatter(whole, 'dp', scatter_dimension=1, tiled=True)  133 us
    unnamed x4, waiting for transfers between devices  32.7 us
    unnamed x42, local copies, waits for them, and re-layouts  26.6 us
    all_to_all x1, waiting for transfers between devices, shards(): lax.all_to_all(outgoing, 'ctx', split_axis=0, concat_axis=0, tiled=True)  18 us
    unnamed x1, blocking collectives  13.1 us
    concatenate x8, local copies, waits for them, and re-layouts, rotate(): jnp.concatenate([first * cosine - second * sine, second * cosine + first...  13 us
    dot_general x1, matrix products, shards(): lax.dot_general(act, slotted, (((0,), (0,)), ((), ())), preferred_element...  10.3 us
    dot_general x1, matrix products, shards(): lax.dot_general(slotted, lax.all_gather(fc2_weight, 'ctx', axis=0, tiled=...  8.01 us
  transfers between devices with their start and end apart: 5, of which 4 were waited for; matrix products, arithmetic and copies ran while one was open for 24% of the time, Pallas kernels for 0%

commit v1 on v0

v1 whole, which is shorter than its diff:
```python
import functools
import math

import jax
import jax.numpy as jnp
from jax import lax
from jax.experimental import pallas as pl
from jax.experimental.pallas import tpu as pltpu
from jax.sharding import PartitionSpec as P

HEAD = 80
WIN = 64
LANES = 128
F32 = jnp.float32
BF16 = jnp.bfloat16


def rope_tables(position):
    quarter = HEAD // 4
    freq = 1.0 / 10000.0 ** (jnp.arange(quarter, dtype=F32) * (4.0 / HEAD))
    rows = position[0].astype(F32)[:, None] * freq[None, :]
    cols = position[1].astype(F32)[:, None] * freq[None, :]
    angles = jnp.concatenate([rows, cols], axis=1)
    cosine, sine = jnp.cos(angles), jnp.sin(angles)
    pad = jnp.zeros((angles.shape[0], LANES - HEAD), F32)
    return (
        jnp.concatenate([cosine, cosine, pad], axis=1),
        jnp.concatenate([-sine, sine, pad], axis=1),
    )


def spread(table, width):
    shape = (LANES, width)
    lane = lax.broadcasted_iota(jnp.int32, shape, 1) % HEAD
    pick = (lane == lax.broadcasted_iota(jnp.int32, shape, 0)).astype(F32).astype(BF16)
    high = table.astype(BF16)
    rest = table - high.astype(F32)
    mid = rest.astype(BF16)
    low = (rest - mid.astype(F32)).astype(BF16)
    dot = functools.partial(jnp.dot, preferred_element_type=F32)
    return dot(high, pick) + dot(mid, pick) + dot(low, pick)


def attention_kernel(q_ref, k_ref, v_ref, g_ref, c_ref, s_ref, dq_ref, dk_ref, dv_ref):
    width = q_ref.shape[1]
    heads = width // HEAD
    half = HEAD // 2
    cosine = spread(c_ref[...], width)
    sine = spread(s_ref[...], width)
    lane = lax.broadcasted_iota(jnp.int32, (WIN, width), 1)
    first = lane % HEAD < half

    def swap(x):
        return jnp.where(first, pltpu.roll(x, width - half, 1), pltpu.roll(x, half, 1))

    def rotated(x):
        return (x * cosine + swap(x) * sine).astype(BF16)

    def unrotated(x):
        return (x * cosine - swap(x) * sine).astype(BF16)

    q = rotated(q_ref[...].astype(F32))
    k = rotated(k_ref[...].astype(F32))
    v = v_ref[...]
    g = g_ref[...]
    factor = HEAD ** (-0.5)
    nt = (((1,), (1,)), ((), ()))
    tn = (((0,), (0,)), ((), ()))
    nn = (((1,), (0,)), ((), ()))

    def dot(a, b, dims):
        return lax.dot_general(a, b, dims, preferred_element_type=F32)

    dq, dk, dv = {}, {}, {}

    def add(into, tile, value):
        for i in range(value.shape[1] // LANES):
            part = value[:, i * LANES : (i + 1) * LANES]
            into[tile + i] = into[tile + i] + part if tile + i in into else part

    for head in range(heads):
        tile = head * HEAD // LANES
        end = -(-(head + 1) * HEAD // LANES)
        lo, hi = tile * LANES, end * LANES
        here = lax.broadcasted_iota(jnp.int32, (1, hi - lo), 1) + lo
        mask = ((here >= head * HEAD) & (here < (head + 1) * HEAD)).astype(F32).astype(BF16)
        qm = q[:, lo:hi] * mask
        km = k[:, lo:hi] * mask
        gm = g[:, lo:hi] * mask
        scores = dot(qm, k[:, lo:hi], nt) * factor
        weight = jnp.exp(scores - jnp.max(scores, axis=1, keepdims=True))
        probs = weight * (1.0 / jnp.sum(weight, axis=1, keepdims=True))
        probs_b = probs.astype(BF16)
        prob_grad = dot(gm, v[:, lo:hi], nt)
        delta = jnp.sum(probs_b.astype(F32) * prob_grad, axis=1, keepdims=True)
        score_grad = (probs * (prob_grad - delta)).astype(BF16)
        add(dv, tile, dot(probs_b, gm, tn))
        add(dq, tile, dot(score_grad, km, nn))
        add(dk, tile, dot(score_grad, qm, tn))

    def joined(parts):
        return jnp.concatenate([parts[i] for i in range(width // LANES)], axis=1)

    dq_ref[...] = unrotated(joined(dq) * factor)
    dk_ref[...] = unrotated(joined(dk) * factor)
    dv_ref[...] = joined(dv).astype(BF16)


def attention_block(query, key_states, value_states, out_grad, position):
    count, width = query.shape
    cosine, sine = rope_tables(position)
    row = pl.BlockSpec((WIN, width), lambda i: (i, 0))
    table = pl.BlockSpec((WIN, LANES), lambda i: (i, 0))
    return pl.pallas_call(
        attention_kernel,
        grid=(count // WIN,),
        in_specs=[row] * 4 + [table] * 2,
        out_specs=[row] * 3,
        out_shape=[jax.ShapeDtypeStruct((count, width), BF16)] * 3,
        cost_estimate=pl.CostEstimate(
            flops=20_000_000_000, bytes_accessed=14 * count * width, transcendentals=0
        ),
        name="attention",
    )(query, key_states, value_states, out_grad, cosine, sine)


def shards(
    merged_grad,
    merged_owner,
    merger_pre,
    fc2_weight,
    query,
    key_states,
    value_states,
    out_grad,
    position,
):
    rows_here = merged_grad.shape[0]
    owners_count = lax.axis_size("ctx")
    replicas = lax.axis_size("dp")
    slots, units = merger_pre.shape
    mine = units // owners_count
    rows = rows_here * owners_count
    places = slots * owners_count
    owner = lax.all_gather(merged_owner[:, 0], "ctx", axis=0, tiled=True)
    merged = lax.all_gather(merged_grad, "ctx", axis=0, tiled=True)
    pre_sent = jnp.transpose(merger_pre.reshape(slots, owners_count, mine), (1, 0, 2))
    pre_got = lax.all_to_all(pre_sent, "ctx", split_axis=0, concat_axis=0, tiled=True)
    pre_got = pre_got.reshape(places, mine)

    attention = attention_block(query, key_states, value_states, out_grad, position)

    peers = jnp.arange(owners_count, dtype=jnp.int32)
    onehot = (peers[:, None] == owner[None, :]).astype(jnp.int32)
    running = jnp.cumsum(onehot, axis=1, dtype=jnp.int32)
    slot = jnp.sum(running * onehot, axis=0, dtype=jnp.int32) - 1
    target = owner * slots + slot
    place = jnp.arange(places, dtype=jnp.int32)
    landing = (place[:, None] == target[None, :]).astype(BF16)

    pre = lax.dot_general(
        landing, pre_got, (((0,), (0,)), ((), ())), preferred_element_type=F32
    )
    cdf = 0.5 * (1.0 + lax.erf(pre * 0.5**0.5))
    act = (pre * cdf).astype(BF16)
    slope = cdf + pre * jnp.exp(-0.5 * pre * pre) * (2.0 * math.pi) ** (-0.5)
    linear = lax.dot_general(
        merged, fc2_weight, (((1,), (1,)), ((), ())), preferred_element_type=F32
    )
    hidden = (linear * slope).astype(BF16)
    hidden_sent = jnp.dot(landing, hidden, preferred_element_type=F32).astype(BF16)
    hidden_got = lax.all_to_all(
        hidden_sent.reshape(owners_count, slots, mine),
        "ctx",
        split_axis=0,
        concat_axis=0,
        tiled=True,
    )
    hidden_grad = jnp.transpose(hidden_got, (1, 0, 2)).reshape(slots, units)
    partial = lax.dot_general(
        act, merged, (((0,), (0,)), ((), ())), preferred_element_type=F32
    )
    summed = lax.psum_scatter(partial, "dp", scatter_dimension=1, tiled=True)
    weight_grad = summed * (rows * replicas) ** (-0.5)
    return (hidden_grad, weight_grad, *attention)


def solution(mesh):
    every = P(("dp", "ctx"), None)
    return jax.shard_map(
        shards,
        mesh=mesh,
        in_specs=(every, every, every, P("ctx", None)) + (every,) * 4 + (P(None, ("dp", "ctx")),),
        out_specs=(every, P("ctx", "dp")) + (every,) * 3,
        check_vma=False,
    )
```

time: 324 us -> 157 us (0.48)
  waiting for transfers between devices: 189 us -> 27.2 us
  local copies, waits for them, and re-layouts: 55.2 us -> 7.84 us
  blocking collectives: 13.1 us -> 50.6 us
  Pallas kernels: 0 us -> 28.4 us
  matrix products: 34.7 us -> 13 us
  starting transfers between devices: 6.99 us -> 11.3 us
  other arithmetic: 7.9 us -> 4.5 us
    reduce_scatter x1 -> x0, waiting for transfers between devices: 133 us -> none  [shards(): partial_dp = lax.psum_scatter(whole, 'dp', scatter_dimension=1, tiled=True)]
    all_gather x0 -> x1, blocking collectives: none -> 50.6 us  [shards(): owner = lax.all_gather(merged_owner[:, 0], 'ctx', axis=0, tiled=True)]
    unnamed x4 -> x3, waiting for transfers between devices: 32.7 us -> 0.7 us
    pallas_call x0 -> x1, Pallas kernels: none -> 28.4 us  [attention_block(): pl.pallas_call(attention_kernel, grid=(count // WIN,), in_specs=[row] * 4...]
    all_gather x1, waiting for transfers between devices: 0.01 us -> 25.4 us  [shards(): merged = lax.all_gather(merged_grad, 'ctx', axis=0, tiled=True)]
    dot_general x9 -> x2, matrix products: 30.1 us -> 7.33 us  [the longest x1 5.63 us: shards(): jnp.dot(landing, hidden, preferred_element_type=F32).astype(BF16)]
    all_to_all x2, waiting for transfers between devices: 23.1 us -> 1.15 us  [the longest x1 1.15 us: shards(): lax.all_to_all(hidden_sent.reshape(owners_count, slots, mine), 'ctx', spl...]
    unnamed x42 -> x11, local copies, waits for them, and re-layouts: 26.6 us -> 6 us
  transfers between devices with their start and end apart: 5 -> 4, of which waited for: 4 -> 2; matrix products, arithmetic and copies ran while one was open for 24% -> 11% of each run, Pallas kernels for 0% -> 18%
where the time goes in v1:
time: 157 us
  blocking collectives  50.6 us (32%)
  Pallas kernels  28.4 us (18%)
  waiting for transfers between devices  27.2 us (17%)
  between operations  14.2 us (9%)
  matrix products  13 us (8%)
  starting transfers between devices  11.3 us (7%)
  local copies, waits for them, and re-layouts  7.84 us (5%)
  other arithmetic  4.5 us (3%)
    all_gather x1, blocking collectives, shards(): owner = lax.all_gather(merged_owner[:, 0], 'ctx', axis=0, tiled=True)  50.6 us
    pallas_call x1, Pallas kernels, attention_block(): pl.pallas_call(attention_kernel, grid=(count // WIN,), in_specs=[row] * 4...  28.4 us
    all_gather x1, waiting for transfers between devices, shards(): merged = lax.all_gather(merged_grad, 'ctx', axis=0, tiled=True)  25.4 us
    all_to_all x1, starting transfers between devices, shards(): lax.all_to_all(pre_sent, 'ctx', split_axis=0, concat_axis=0, tiled=True)  7.44 us
    unnamed x11, local copies, waits for them, and re-layouts  6 us
    unnamed x1, matrix products  5.69 us
    dot_general x1, matrix products, shards(): jnp.dot(landing, hidden, preferred_element_type=F32).astype(BF16)  5.63 us
    all_to_all x1, starting transfers between devices, shards(): lax.all_to_all(hidden_sent.reshape(owners_count, slots, mine), 'ctx', spl...  3.75 us
  transfers between devices with their start and end apart: 4, of which 2 were waited for; matrix products, arithmetic and copies ran while one was open for 11% of the time, Pallas kernels for 18%

profile of v1, /device:TPU:0, one launch (start us, length us, event | category | flops | bytes accessed | tf_op | source)
XLA Modules:
  0.0 157.0 jit_solution(18017473151692421919)
XLA Ops:
  7.2 0.7 all-gather.3.cloned.1.call-update
  7.9 2.4 %copy.25 = bf16[256,2560]{0,1:T(8,128)(2,1)} copy(bf16[256,2560]{1,0:T(8,128)(2,1)} %param.11) | data formatting | bytes 2621440 | tf_op args[2]
  10.3 7.4 %all-to-all-start = ((bf16[8,256,320]{1,2,0:T(8,128)(2,1)}), bf16[8,256,320]{1,2,0:T(8,128)(2,1)S(1)}, u32[]{:S(2)}, u32[]{:S(2)}) async-start(bf16[8,256,320]{1,2,0:T(8,128)(2,1)} %bitcast.29), calls=%async_computation | async-start | bytes 2621440 | tf_op jit(solution)/shard_map/all_to_all | solution.py:148
  17.8 50.6 %all-gather = s32[1024,1]{0,1:T(1,128)S(1)} all-gather(s32[128,1]{0,1:T(1,128)S(1)} %copy-done.2), channel_id=2, replica_groups=mesh['dp'=4,'ctx'=8] {'ctx'}, dimensions={0}, use_global_device_ids=true | all-gather | bytes 4608 | tf_op jit(solution)/shard_map/all_gather | solution.py:145
  68.4 2.3 %reduce-window.6 = s32[8,8,128]{2,1,0:T(8,128)S(1)} reduce-window(s32[8,8,128]{2,1,0:T(8,128)S(1)} %fusion.10, s32[]{:T(128)} %constant.13.clone.1), window={size=1x1x128 pad=0_0x0_0x127_0}, to_apply=%region_0.0 | reduce-window | flops 1040384 | bytes 65540 | tf_op jit(solution)/shard_map/reduce-window
  70.7 0.3 slice_reduce_fusion
  71.0 0.2 reduce-window.9
  71.3 0.2 copy.36
  71.4 1.7 %fusion.1 = f32[1024,320]{0,1:T(8,128)S(1)} fusion(bf16[2048,320]{0,1:T(8,128)(2,1)S(1)} %bitcast.31, s32[1024]{0:T(1024)S(1)} %bitcast_add_fusion), kind=kOutput, calls=%fused_computation.2 | convolution fusion | flops 1344274432 | bytes 2625536 | tf_op jit(solution)/shard_map/dot_general | solution.py:161
  73.1 25.4 %all-gather.3.cloned.1.call-done = bf16[1024,1792]{1,0:T(8,128)(2,1)} async-done(((bf16[128,1792]{1,0:T(8,128)(2,1)}), bf16[1024,1792]{1,0:T(8,128)(2,1)}) %all-gather.3.cloned.1.call-update) | async-done | bytes 3670032 | tf_op jit(solution)/shard_map/all_gather | solution.py:146
  98.5 5.7 %convolution_bitcast_fusion = f32[1792,320]{1,0:T(8,128)} fusion(bf16[1024,1792]{1,0:T(8,128)(2,1)} %all-gather.3.cloned.1.call-done, f32[1024,320]{0,1:T(8,128)S(1)} %fusion.1), kind=kOutput, calls=%fused_computation.5 | convolution fusion | flops 1176043520 | bytes 7274496
  104.3 0.6 copy-done.1
  104.9 5.6 %fusion.4 = bf16[2048,320]{0,1:T(8,128)(2,1)S(1)} fusion(s32[1024]{0:T(1024)S(1)} %bitcast_add_fusion, bf16[1024,1792]{1,0:T(8,128)(2,1)} %all-gather.3.cloned.1.call-done, bf16[320,1792]{1,0:T(8,128)(2,1)S(1)} %copy-done, f32[1024,320]{0,1:T(8,128)} %copy-done.3), kind=kOutput, calls=%fused_computation.6 | convolution fusion | flops 2522611712 | bytes 7442432 | tf_op jit(solution)/shard_map/dot_general | solution.py:171
  110.5 1.1 copy.38
  111.7 3.8 %all-to-all-start.1 = ((bf16[8,256,320]{1,2,0:T(8,128)(2,1)}), bf16[8,256,320]{1,2,0:T(8,128)(2,1)S(1)}, u32[]{:S(2)}, u32[]{:S(2)}) async-start(bf16[8,256,320]{1,2,0:T(8,128)(2,1)} %bitcast.27), calls=%async_computation.1 | async-start | bytes 2621440 | tf_op jit(solution)/shard_map/all_to_all | solution.py:172
  115.5 0.2 fusion.11
  115.7 0.1 copy.30
  115.8 0.1 copy.28
  116.0 0.8 maximum_maximum_fusion.1
  116.8 28.4 %attention.1 = (bf16[256,1280]{1,0:T(8,128)(2,1)}, bf16[256,1280]{1,0:T(8,128)(2,1)}, bf16[256,1280]{1,0:T(8,128)(2,1)}) custom-call(bf16[256,1280]{1,0:T(8,128)(2,1)} %q_ref.1, bf16[256,1280]{1,0:T(8,128)(2,1)} %k_ref.1, bf16[256,1280]{1,0:T(8,128)(2,1)} %v_ref.1, bf16[256,1280]{1,0:T(8,128)(2,1)} %g_ref.1, f32[256,128]{1,0:T(8,128)} %get-tuple-element.31.c_ref, ...), custom_call_target="tpu_custom_call" | custom-call | flops 20000000000 | bytes 4587520 | tf_op jit(solution)/shard_map/attention/pallas_call | solution.py:114
  145.2 1.1 all-to-all-done.1
  146.3 1.6 %copy.32 = bf16[256,2560]{1,0:T(8,128)(2,1)} copy(bf16[256,2560]{0,1:T(8,128)(2,1)S(1)} %bitcast.26) | data formatting | bytes 2621440
  147.9 1.3 copy.34
  149.3 0.9 broadcast_multiply_fusion
  (22 shorter events, 0.4 us)
Async XLA Ops:
  7.2 97.7 %copy-start = (bf16[320,1792]{1,0:T(8,128)(2,1)S(1)}, bf16[320,1792]{1,0:T(8,128)(2,1)}, u32[]{:S(2)}) copy-start(bf16[320,1792]{1,0:T(8,128)(2,1)} %param.12) | copy-start | bytes 3440644
  7.2 91.3 %all-gather.3.cloned.1.call-start = ((), (), s32[]{:S(2)}) async-start(), calls=%async_computation.3 | async-start | bytes 4128768 | tf_op jit(solution)/shard_map/all_gather | solution.py:146
  10.3 7.5 %copy-start.2 = (s32[128,1]{0,1:T(1,128)S(1)}, s32[128,1]{0,1:T(1,128)}, u32[]{:S(2)}) copy-start(s32[128,1]{0,1:T(1,128)} %param.10) | copy-start | bytes 1540
  10.3 60.9 %all-to-all-start = ((bf16[8,256,320]{1,2,0:T(8,128)(2,1)}), bf16[8,256,320]{1,2,0:T(8,128)(2,1)S(1)}, u32[]{:S(2)}, u32[]{:S(2)}) async-start(bf16[8,256,320]{1,2,0:T(8,128)(2,1)} %bitcast.29), calls=%async_computation | async-start | bytes 2621440 | tf_op jit(solution)/shard_map/all_to_all | solution.py:148
  17.8 130.1 %reduce-scatter.4.cloned.1.call-start = ((), (), s32[]{:S(2)}) async-start(), calls=%async_computation.4 | async-start | bytes 3440640
  73.1 31.1 %copy-start.3 = (f32[1024,320]{0,1:T(8,128)}, f32[1024,320]{0,1:T(8,128)S(1)}, u32[]{:S(2)}) copy-start(f32[1024,320]{0,1:T(8,128)S(1)} %fusion.1) | copy-start | bytes 3932164
  104.2 0.7 copy-start.1
  111.7 34.7 %all-to-all-start.1 = ((bf16[8,256,320]{1,2,0:T(8,128)(2,1)}), bf16[8,256,320]{1,2,0:T(8,128)(2,1)S(1)}, u32[]{:S(2)}, u32[]{:S(2)}) async-start(bf16[8,256,320]{1,2,0:T(8,128)(2,1)} %bitcast.27), calls=%async_computation.1 | async-start | bytes 2621440 | tf_op jit(solution)/shard_map/all_to_all | solution.py:172
Sparse Core Ops, SparseCore 0:
  10.2 88.3 all-gather.2
  104.4 34.0 reduce-scatter.3

commit v2 on v1

v2 whole, which is shorter than its diff:
```python
import functools
import math

import jax
import jax.numpy as jnp
from jax import lax
from jax.experimental import pallas as pl
from jax.experimental.pallas import tpu as pltpu
from jax.sharding import PartitionSpec as P

HEAD = 80
WIN = 64
LANES = 128
F32 = jnp.float32
BF16 = jnp.bfloat16
MESH = pl.DeviceIdType.MESH


def rope_tables(position):
    quarter = HEAD // 4
    freq = 1.0 / 10000.0 ** (jnp.arange(quarter, dtype=F32) * (4.0 / HEAD))
    rows = position[0].astype(F32)[:, None] * freq[None, :]
    cols = position[1].astype(F32)[:, None] * freq[None, :]
    angles = jnp.concatenate([rows, cols], axis=1)
    cosine, sine = jnp.cos(angles), jnp.sin(angles)
    pad = jnp.zeros((angles.shape[0], LANES - HEAD), F32)
    return (
        jnp.concatenate([cosine, cosine, pad], axis=1),
        jnp.concatenate([-sine, sine, pad], axis=1),
    )


def spread(table, width):
    shape = (LANES, width)
    lane = lax.broadcasted_iota(jnp.int32, shape, 1) % HEAD
    pick = (lane == lax.broadcasted_iota(jnp.int32, shape, 0)).astype(F32).astype(BF16)
    high = table.astype(BF16)
    rest = table - high.astype(F32)
    mid = rest.astype(BF16)
    low = (rest - mid.astype(F32)).astype(BF16)
    dot = functools.partial(jnp.dot, preferred_element_type=F32)
    return dot(high, pick) + dot(mid, pick) + dot(low, pick)


def attention_window(w, q_ref, k_ref, v_ref, g_ref, c_ref, s_ref, dq_ref, dk_ref, dv_ref):
    at = pl.ds(pl.multiple_of(w * WIN, WIN), WIN)
    width = q_ref.shape[1]
    heads = width // HEAD
    half = HEAD // 2
    cosine = spread(c_ref[at, :], width)
    sine = spread(s_ref[at, :], width)
    lane = lax.broadcasted_iota(jnp.int32, (WIN, width), 1)
    first = lane % HEAD < half

    def swap(x):
        return jnp.where(first, pltpu.roll(x, width - half, 1), pltpu.roll(x, half, 1))

    def rotated(x):
        return (x * cosine + swap(x) * sine).astype(BF16)

    def unrotated(x):
        return (x * cosine - swap(x) * sine).astype(BF16)

    q = rotated(q_ref[at, :].astype(F32))
    k = rotated(k_ref[at, :].astype(F32))
    v = v_ref[at, :]
    g = g_ref[at, :]
    factor = HEAD ** (-0.5)
    nt = (((1,), (1,)), ((), ()))
    tn = (((0,), (0,)), ((), ()))
    nn = (((1,), (0,)), ((), ()))

    def dot(a, b, dims):
        return lax.dot_general(a, b, dims, preferred_element_type=F32)

    dq, dk, dv = {}, {}, {}

    def add(into, tile, value):
        for i in range(value.shape[1] // LANES):
            part = value[:, i * LANES : (i + 1) * LANES]
            into[tile + i] = into[tile + i] + part if tile + i in into else part

    for head in range(heads):
        tile = head * HEAD // LANES
        end = -(-(head + 1) * HEAD // LANES)
        lo, hi = tile * LANES, end * LANES
        here = lax.broadcasted_iota(jnp.int32, (1, hi - lo), 1) + lo
        mask = ((here >= head * HEAD) & (here < (head + 1) * HEAD)).astype(F32).astype(BF16)
        qm = q[:, lo:hi] * mask
        km = k[:, lo:hi] * mask
        gm = g[:, lo:hi] * mask
        scores = dot(qm, k[:, lo:hi], nt) * factor
        weight = jnp.exp(scores - jnp.max(scores, axis=1, keepdims=True))
        probs = weight * (1.0 / jnp.sum(weight, axis=1, keepdims=True))
        probs_b = probs.astype(BF16)
        prob_grad = dot(gm, v[:, lo:hi], nt)
        delta = jnp.sum(probs_b.astype(F32) * prob_grad, axis=1, keepdims=True)
        score_grad = (probs * (prob_grad - delta)).astype(BF16)
        add(dv, tile, dot(probs_b, gm, tn))
        add(dq, tile, dot(score_grad, km, nn))
        add(dk, tile, dot(score_grad, qm, tn))

    def joined(parts):
        return jnp.concatenate([parts[i] for i in range(width // LANES)], axis=1)

    dq_ref[at, :] = unrotated(joined(dq) * factor)
    dk_ref[at, :] = unrotated(joined(dk) * factor)
    dv_ref[at, :] = joined(dv).astype(BF16)


def fused_kernel(
    owners_count,
    replicas,
    m_ref,
    o_ref,
    p_ref,
    w_ref,
    q_ref,
    k_ref,
    v_ref,
    g_ref,
    c_ref,
    s_ref,
    h_out,
    wg_out,
    dq_ref,
    dk_ref,
    dv_ref,
    mall,
    owners,
    pre_got,
    code,
    act,
    hid,
    hid_out,
    full,
    part,
    part_got,
    m_recv,
    up_sem,
    down_sem,
    side_sem,
    o_send,
    o_recv,
    p_send,
    p_recv,
    h_send,
    h_recv,
    r_send,
    r_recv,
    local_sem,
):
    n = owners_count
    sides = 2
    line = n // sides
    rows_here = m_ref.shape[0]
    mine, slots = pre_got.shape[1:]
    block = sides * rows_here
    blocks = n // sides
    windows = q_ref.shape[0] // WIN
    me = lax.axis_index("ctx")
    rep = lax.axis_index("dp")
    a, b = me // sides, me % sides

    barrier = pltpu.get_barrier_semaphore()
    for r in range(1, n):
        pl.semaphore_signal(barrier, inc=1, device_id={"dp": rep, "ctx": (me + r) % n}, device_id_type=MESH)
    for r in range(1, replicas):
        pl.semaphore_signal(
            barrier, inc=1, device_id={"dp": (rep + r) % replicas, "ctx": me}, device_id_type=MESH
        )
    pl.semaphore_wait(barrier, n - 1 + replicas - 1)

    def send(src, dst, send_sem, recv_sem, ctx=None, dp=None):
        where = {"dp": rep if dp is None else dp, "ctx": me if ctx is None else ctx}
        return pltpu.make_async_remote_copy(
            src_ref=src,
            dst_ref=dst,
            send_sem=send_sem,
            recv_sem=recv_sem,
            device_id=where,
            device_id_type=MESH,
        )

    def owner_copy(r):
        return send(o_ref, owners.at[me], o_send.at[r - 1], o_recv.at[r - 1], ctx=(me + r) % n)

    def pre_copy(r):
        peer = (me + r) % n
        return send(p_ref.at[peer], pre_got.at[me], p_send.at[r - 1], p_recv.at[r - 1], ctx=peer)

    def hidden_copy(r):
        peer = (me + r) % n
        return send(hid_out.at[peer], h_out.at[me], h_send.at[r - 1], h_recv.at[r - 1], ctx=peer)

    def part_copy(r):
        peer = (rep + r) % replicas
        return send(part.at[peer], part_got.at[r - 1], r_send.at[r - 1], r_recv.at[r - 1], dp=peer)

    def up_copy(t, ref):
        return send(ref, mall.at[(a - t) * sides + b], up_sem.at[t], m_recv.at[(a - t) * sides + b], ctx=me + sides)

    def down_copy(t, ref):
        return send(ref, mall.at[(a + t) * sides + b], down_sem.at[t], m_recv.at[(a + t) * sides + b], ctx=me - sides)

    def side_copy(at, ref):
        return send(ref, mall.at[at * sides + b], side_sem.at[at], m_recv.at[at * sides + b], ctx=a * sides + 1 - b)

    def arrived(src):
        send(mall.at[src], mall.at[src], up_sem.at[0], m_recv.at[src], ctx=a * sides + 1 - b).wait_recv()

    for r in range(1, n):
        owner_copy(r).start()

    @pl.when(a + 1 < line)
    def _():
        up_copy(0, m_ref).start()

    @pl.when(a > 0)
    def _():
        down_copy(0, m_ref).start()

    side_copy(a, m_ref).start()
    for r in range(1, n):
        pre_copy(r).start()
    locals_ = [
        pltpu.make_async_copy(m_ref, mall.at[me], local_sem.at[0]),
        pltpu.make_async_copy(o_ref, owners.at[me], local_sem.at[1]),
        pltpu.make_async_copy(p_ref.at[me], pre_got.at[me], local_sem.at[2]),
    ]
    for copy in locals_:
        copy.start()

    def forward(t):
        @pl.when(a - t >= 0)
        def _():
            ref = mall.at[(a - t) * sides + b]
            arrived((a - t) * sides + b)

            @pl.when(a + 1 < line)
            def _():
                up_copy(t, ref).start()

            side_copy(a - t, ref).start()

        @pl.when(a + t < line)
        def _():
            ref = mall.at[(a + t) * sides + b]
            arrived((a + t) * sides + b)

            @pl.when(a > 0)
            def _():
                down_copy(t, ref).start()

            side_copy(a + t, ref).start()

    def with_window(w, carry):
        attention_window(w, q_ref, k_ref, v_ref, g_ref, c_ref, s_ref, dq_ref, dk_ref, dv_ref)

        @pl.when(w + 1 < line)
        def _():
            forward(w + 1)

        return carry

    lax.fori_loop(0, windows, with_window, 0)

    def only_forward(t, carry):
        forward(t)
        return carry

    if windows + 1 < line:
        lax.fori_loop(windows + 1, line, only_forward, 0)

    for copy in locals_:
        copy.wait()
    for r in range(1, n):
        owner_copy(r).wait()

    padded = -(-n // 16) * 16
    earlier = lax.broadcasted_iota(jnp.int32, (rows_here, rows_here), 0) < lax.broadcasted_iota(
        jnp.int32, (rows_here, rows_here), 1
    )
    earlier = earlier.astype(F32).astype(BF16)
    names = lax.broadcasted_iota(jnp.int32, (padded, rows_here), 0)
    base = jnp.zeros((padded, 1), F32)
    for s in range(n):
        onehot = (names == owners[s, 0:1, :]).astype(F32)
        count = jnp.dot(onehot.astype(BF16), earlier, preferred_element_type=F32) + base
        place = jnp.sum(onehot * (count + names.astype(F32) * float(slots)), axis=0, keepdims=True)
        base = base + jnp.sum(onehot, axis=1, keepdims=True)
        lo = s % sides * rows_here
        code[s // sides, :, lo : lo + rows_here] = jnp.broadcast_to(place, (8, rows_here))

    for r in range(1, n):
        pre_copy(r).wait()
    for src in range(line):
        arrived(src * sides + 1 - b)

    standing = lax.broadcasted_iota(jnp.int32, (slots, block), 0).astype(F32)

    def landing(o, t):
        first = (o * slots).astype(F32)
        return (standing == code[t, 0:1, :] - first).astype(F32).astype(BF16)

    def tokens(t, carry):
        def gather(o, total):
            return total + jnp.dot(pre_got[o], landing(o, t), preferred_element_type=F32)

        pre = lax.fori_loop(0, n, gather, jnp.zeros((mine, block), F32))
        cdf = 0.5 * (1.0 + lax.erf(pre * 0.5**0.5))
        slope = cdf + pre * jnp.exp(-0.5 * pre * pre) * (2.0 * math.pi) ** (-0.5)
        rows = jnp.concatenate([mall[t * sides + i] for i in range(sides)], axis=0)
        linear = lax.dot_general(
            w_ref[...], rows, (((1,), (1,)), ((), ())), preferred_element_type=F32
        )
        act[t] = (pre * cdf).astype(BF16)
        hid[t] = (linear * slope).astype(BF16)
        return carry

    lax.fori_loop(0, blocks, tokens, 0)

    def outgoing(o, carry):
        def gather(t, total):
            return total + lax.dot_general(
                hid[t], landing(o, t), (((1,), (1,)), ((), ())), preferred_element_type=F32
            )

        hid_out[o] = lax.fori_loop(0, blocks, gather, jnp.zeros((mine, slots), F32)).astype(BF16)
        return carry

    lax.fori_loop(0, n, outgoing, 0)
    for r in range(1, n):
        hidden_copy(r).start()
    own = pltpu.make_async_copy(hid_out.at[me], h_out.at[me], local_sem.at[3])
    own.start()

    width = full.shape[1]

    def partial(t, carry):
        rows = jnp.concatenate([mall[t * sides + i] for i in range(sides)], axis=0)
        full[...] += jnp.dot(act[t], rows, preferred_element_type=F32)
        return carry

    full[...] = jnp.zeros_like(full)
    lax.fori_loop(0, blocks, partial, 0)
    piece = width // replicas
    for d in range(replicas):
        lo = d * piece // LANES * LANES
        hi = -(-(d + 1) * piece // LANES) * LANES
        shift = d * piece - lo
        value = full[:, lo:hi]
        if shift:
            value = pltpu.roll(value, hi - lo - shift, 1)
        part[d] = value[:, :piece]
    for r in range(1, replicas):
        part_copy(r).start()
    for r in range(1, replicas):
        part_copy(r).wait()
    total = part[rep]
    for r in range(1, replicas):
        total = total + part_got[r - 1]
    wg_out[...] = total

    own.wait()
    for r in range(1, n):
        hidden_copy(r).wait()

    def sent(t, carry):
        @pl.when((a - t >= 0) & (a + 1 < line))
        def _():
            up_copy(t, mall.at[me]).wait_send()

        @pl.when((a + t < line) & (a > 0))
        def _():
            down_copy(t, mall.at[me]).wait_send()

        side_copy(t, mall.at[me]).wait_send()
        return carry

    lax.fori_loop(0, line, sent, 0)


def fused(merged_grad, merged_owner, merger_pre, fc2_weight, query, key_states, value_states, out_grad, position):
    rows_here, width = merged_grad.shape
    n, replicas = lax.axis_size("ctx"), lax.axis_size("dp")
    slots, units = merger_pre.shape
    mine = units // n
    block, blocks = 2 * rows_here, n // 2
    piece = width // replicas
    cosine, sine = rope_tables(position)
    pre = jnp.transpose(merger_pre).reshape(n, mine, slots)
    owner = jnp.broadcast_to(merged_owner.reshape(1, rows_here), (8, rows_here))
    vmem = pl.BlockSpec(memory_space=pltpu.VMEM)
    dma = pltpu.SemaphoreType.DMA
    like = jax.ShapeDtypeStruct(query.shape, BF16)
    hidden, weight, *attention = pl.pallas_call(
        functools.partial(fused_kernel, n, replicas),
        in_specs=[vmem] * 10,
        out_specs=[vmem] * 5,
        out_shape=[
            jax.ShapeDtypeStruct((n, mine, slots), BF16),
            jax.ShapeDtypeStruct((mine, piece), F32),
            like,
            like,
            like,
        ],
        scratch_shapes=[
            pltpu.VMEM((n, rows_here, width), BF16),
            pltpu.VMEM((n, 8, rows_here), jnp.int32),
            pltpu.VMEM((n, mine, slots), BF16),
            pltpu.VMEM((blocks, 8, block), F32),
            pltpu.VMEM((blocks, mine, block), BF16),
            pltpu.VMEM((blocks, mine, block), BF16),
            pltpu.VMEM((n, mine, slots), BF16),
            pltpu.VMEM((mine, width), F32),
            pltpu.VMEM((replicas, mine, piece), F32),
            pltpu.VMEM((replicas - 1, mine, piece), F32),
            dma((n,)),
            dma((blocks,)),
            dma((blocks,)),
            dma((blocks,)),
            dma((n - 1,)),
            dma((n - 1,)),
            dma((n - 1,)),
            dma((n - 1,)),
            dma((n - 1,)),
            dma((n - 1,)),
            dma((replicas - 1,)),
            dma((replicas - 1,)),
            dma((4,)),
        ],
        compiler_params=pltpu.CompilerParams(
            collective_id=0, has_side_effects=True, vmem_limit_bytes=60 * 2**20
        ),
        name="fused",
    )(merged_grad, owner, pre, fc2_weight, query, key_states, value_states, out_grad, cosine, sine)
    hidden_grad = jnp.transpose(hidden.reshape(units, slots))
    weight_grad = weight * (rows_here * n * replicas) ** (-0.5)
    return (hidden_grad, weight_grad, *attention)


def solution(mesh):
    every = P(("dp", "ctx"), None)
    return jax.shard_map(
        fused,
        mesh=mesh,
        in_specs=(every, every, every, P("ctx", None)) + (every,) * 4 + (P(None, ("dp", "ctx")),),
        out_specs=(every, P("ctx", "dp")) + (every,) * 3,
        check_vma=False,
    )
```

time: 157 us -> 142 us (0.904)
  Pallas kernels: 28.4 us -> 130 us
  blocking collectives: 50.6 us -> 0 us
  waiting for transfers between devices: 27.2 us -> 0 us
  between operations: 14.2 us -> 0.69 us
  matrix products: 13 us -> 0 us
  starting transfers between devices: 11.3 us -> 0 us
  other arithmetic: 4.5 us -> 2.78 us
    pallas_call x1, Pallas kernels: 28.4 us -> 130 us  [fused(): pl.pallas_call(functools.partial(fused_kernel, n, replicas), in_specs=[vm...]
    all_gather x1 -> x0, blocking collectives: 50.6 us -> none  [shards(): owner = lax.all_gather(merged_owner[:, 0], 'ctx', axis=0, tiled=True)]
    all_gather x1 -> x0, waiting for transfers between devices: 25.4 us -> none  [shards(): merged = lax.all_gather(merged_grad, 'ctx', axis=0, tiled=True)]
    all_to_all x2 -> x0, starting transfers between devices: 11.2 us -> none  [the longest x1 7.44 us: shards(): lax.all_to_all(pre_sent, 'ctx', split_axis=0, concat_axis=0, tiled=True)]
    dot_general x2 -> x0, matrix products: 7.33 us -> none  [the longest x1 5.63 us: shards(): jnp.dot(landing, hidden, preferred_element_type=F32).astype(BF16)]
    unnamed x1 -> x0, matrix products: 5.69 us -> none
    unnamed x11 -> x13, local copies, waits for them, and re-layouts: 6 us -> 2.95 us
    another operation x2 -> x0, other arithmetic: 2.41 us -> none
  transfers between devices with their start and end apart: 4 -> 0, of which waited for: 2 -> 0; matrix products, arithmetic and copies ran while one was open for 11% -> 0% of each run, Pallas kernels for 18% -> 0%
where the time goes in v2:
time: 142 us
  Pallas kernels  130 us (92%)
  local copies, waits for them, and re-layouts  8.38 us (6%)
  other arithmetic  2.78 us (2%)
    pallas_call x1, Pallas kernels, fused(): pl.pallas_call(functools.partial(fused_kernel, n, replicas), in_specs=[vm...  130 us
    unnamed x13, local copies, waits for them, and re-layouts  2.95 us

profile of v2, /device:TPU:0, one launch (start us, length us, event | category | flops | bytes accessed | tf_op | source)
XLA Modules:
  0.0 141.6 jit_solution(4514977687650986254)
XLA Ops:
  0.6 0.0 copy-start
  0.7 0.1 pad.5.clone
  0.7 0.8 slice_convert_fusion.1
  1.5 1.2 broadcast_in_dim.7.o_ref
  2.8 0.1 broadcast_multiply_fusion.2
  2.8 0.2 fusion
  3.0 0.1 copy.23
  3.1 0.1 copy.21
  3.2 0.8 maximum_maximum_fusion.1
  4.1 0.0 copy-done
  4.1 1.4 %copy.20 = bf16[2560,256]{1,0:T(8,128)(2,1)} copy(bf16[2560,256]{0,1:T(8,128)(2,1)S(1)} %bitcast.8) | data formatting | bytes 2621440 | tf_op jit(solution)/shard_map/transpose | solution.py:392
  5.5 129.7 %fused.1 = (bf16[8,320,256]{2,1,0:T(8,128)(2,1)}, f32[320,448]{1,0:T(8,128)}, bf16[256,1280]{1,0:T(8,128)(2,1)}, bf16[256,1280]{1,0:T(8,128)(2,1)}, bf16[256,1280]{1,0:T(8,128)(2,1)}) custom-call(bf16[128,1792]{1,0:T(8,128)(2,1)} %m_ref.1, s32[8,128]{1,0:T(8,128)} %broadcast_in_dim.7.o_ref, bf16[8,320,256]{2,1,0:T(8,128)(2,1)} %bitcast.7, ...), custom_call_target="tpu_custom_call" | custom-call | tf_op jit(solution)/shard_map/fused/pallas_call | solution.py:397
  135.2 0.0 copy-start.4
  135.2 2.5 %copy.25 = bf16[2560,256]{0,1:T(8,128)(2,1)} copy(bf16[2560,256]{1,0:T(8,128)(2,1)} %bitcast.10) | data formatting | bytes 2621440 | tf_op jit(solution)/shard_map/reshape | solution.py:438
  137.7 0.0 copy-start.3
  137.7 0.0 copy-done.4
  137.7 0.0 copy-start.2
  137.7 0.9 broadcast_multiply_fusion
  138.6 0.4 copy-done.3
  139.1 0.8 copy.29
  139.9 0.0 copy-done.2
  139.9 0.8 copy.30
  140.7 0.0 copy-done.1
  140.7 0.8 copy.31
  (4 shorter events, 0.0 us)
Async XLA Ops:
  0.6 3.4 %copy-start = (bf16[256,2560]{1,0:T(8,128)(2,1)S(1)}, bf16[256,2560]{1,0:T(8,128)(2,1)}, u32[]{:S(2)}) copy-start(bf16[256,2560]{1,0:T(8,128)(2,1)} %param.11) | copy-start | bytes 3932164
  135.2 2.5 %copy-start.4 = (f32[320,448]{1,0:T(8,128)S(1)}, f32[320,448]{1,0:T(8,128)}, u32[]{:S(2)}) copy-start(f32[320,448]{1,0:T(8,128)} %get-tuple-element.11) | copy-start | bytes 1720324
  137.7 1.3 copy-start.3
  137.7 2.2 %copy-start.2 = (bf16[256,1280]{1,0:T(8,128)(2,1)S(1)}, bf16[256,1280]{1,0:T(8,128)(2,1)}, u32[]{:S(2)}) copy-start(bf16[256,1280]{1,0:T(8,128)(2,1)} %get-tuple-element.31) | copy-start | bytes 1966084
  139.1 1.7 %copy-start.1 = (bf16[256,1280]{1,0:T(8,128)(2,1)S(1)}, bf16[256,1280]{1,0:T(8,128)(2,1)}, u32[]{:S(2)}) copy-start(bf16[256,1280]{1,0:T(8,128)(2,1)} %get-tuple-element.32) | copy-start | bytes 1966084
